TPU v7x, 32 devices: a whole 2x2x4 slice. The times are simulated.
32 devices in a mesh: shard: 4 (over z), ctx: 2 (over x), tp: 4 (over y, core).
Axes of the slice: x: 2, y: 2, z: 4, core: 2. Of those that a mesh axis runs over, the one named last changes fastest.
Arguments:
- activations: bfloat16 [4, 1040, 768], P('shard', 'ctx'), may hold values from -6 to 6
- slot_counts: int32 [4, 2], P('shard'), may hold values from 1 to 520, as said below
- qkv_weight: bfloat16 [3, 768, 768], P(None, 'shard', 'tp'), may hold values from -0.21875 to 0.21875
- proj_weight: bfloat16 [768, 768], P('tp', 'shard'), may hold values from -3 to 3
- up_weight: bfloat16 [768, 3072], P('shard', 'tp'), may hold values from -0.21875 to 0.21875
- down_weight: bfloat16 [3072, 768], P('tp', 'shard'), may hold values from -0.109375 to 0.109375
- norm_gains: bfloat16 [2, 768], P(None, 'shard'), may hold values from 0.5 to 1.5
- row_biases: bfloat16 [4, 768], P(None, 'shard'), may hold values from -3 to 3
- head_biases: bfloat16 [2, 768], P(None, 'tp'), may hold values from -0.59765625 to 0.59765625
- hidden_bias: bfloat16 [3072], P('tp'), may hold values from -3 to 3
- cotangent: bfloat16 [4, 1040, 768], P('shard', 'ctx'), may hold values from -6 to 6
Outputs:
- layer_out: bfloat16 [4, 1040, 768], P('shard', ('ctx', 'tp'))
- input_grad: bfloat16 [4, 1040, 768], P('shard', ('ctx', 'tp'))
- qkv_weight_grad: float32 [3, 768, 768], P(None, 'shard', 'tp')
- proj_weight_grad: float32 [768, 768], P('tp', 'shard')
- up_weight_grad: float32 [768, 3072], P('shard', 'tp')
- down_weight_grad: float32 [3072, 768], P('tp', 'shard')
- norm_gains_grad: float32 [2, 768], P(None, 'shard')
- row_biases_grad: float32 [4, 768], P(None, 'shard')
- head_biases_grad: float32 [2, 768], P(None, 'tp')
- hidden_bias_grad: float32 [3072], P('tp')
Inputs may be any that keep to these rules, and one draw needn't show every extreme that they name: Row b splits image b's 1025 tokens over the indices of ctx: slot_counts[b, r] of them lie in the first slots of index r's 520; each row sums to 1025; in each row one index holds exactly 520 and the others share the rest as evenly as possible.
All inputs are finite; a program needn't handle non-finite values.
Results may differ from a plain program's by a relative error of at most 0.012.
Values may be sent and summed in bfloat16 or wider, within the bound.
No kernel may reach another device: no remote copies, remote signals or barrier semaphores. Data moves between devices by JAX's collectives and lax.ppermute only.
A program may use at most 64 MiB of HBM per device.

v0:
```python
import math
import jax
import jax.numpy as jnp
from jax import lax
from jax.sharding import PartitionSpec as P

HD = 64
EPS = 1e-06
NEG = -1e30


def layer_norm(values, gain, shift):
    centred = values - jnp.mean(values, axis=-1, keepdims=True)
    spread = jnp.mean(centred * centred, axis=-1, keepdims=True)
    return centred * lax.rsqrt(spread + EPS) * gain + shift


def exact_gelu(hidden):
    return jax.nn.gelu(hidden, approximate=False)


def head_scores(queries, keys, keep):
    scale = 1.0 / math.sqrt(HD)
    scores = jnp.einsum("qhd,khd->hqk", queries, keys, preferred_element_type=jnp.float32) * scale
    return jnp.where(keep[None, None, :], scores, NEG)


def attend(item):
    queries, keys, values, keep = item
    slot_total = queries.shape[0]
    query_heads = queries.reshape(slot_total, -1, HD)
    key_heads = keys.reshape(keys.shape[0], -1, HD)
    value_heads = values.reshape(values.shape[0], -1, HD)
    scores = head_scores(query_heads, key_heads, keep)
    peak = jnp.max(scores, axis=-1, keepdims=True)
    log_total = peak + jnp.log(jnp.sum(jnp.exp(scores - peak), axis=-1, keepdims=True))
    attn_weights = jnp.exp(scores - log_total).astype(jnp.bfloat16)
    mixed = jnp.einsum(
        "hqk,khd->qhd", attn_weights, value_heads, preferred_element_type=jnp.float32
    )
    return (mixed.reshape(slot_total, -1).astype(jnp.bfloat16), log_total)


def attend_back(item):
    queries, keys, values, keep, log_total, grad_mixed = item
    scale = 1.0 / math.sqrt(HD)
    slot_total = queries.shape[0]
    key_total = keys.shape[0]
    query_heads = queries.reshape(slot_total, -1, HD)
    key_heads = keys.reshape(key_total, -1, HD)
    value_heads = values.reshape(key_total, -1, HD)
    grad_heads = grad_mixed.reshape(slot_total, -1, HD)
    scores = head_scores(query_heads, key_heads, keep)
    attn_weights = jnp.exp(scores - log_total)
    weights_low = attn_weights.astype(jnp.bfloat16)
    grad_weights = jnp.einsum(
        "qhd,khd->hqk", grad_heads, value_heads, preferred_element_type=jnp.float32
    )
    grad_values = jnp.einsum(
        "hqk,qhd->khd", weights_low, grad_heads, preferred_element_type=jnp.float32
    )
    inner = jnp.sum(grad_weights * attn_weights, axis=-1, keepdims=True)
    grad_scores = (attn_weights * (grad_weights - inner)).astype(jnp.bfloat16)
    grad_queries = (
        jnp.einsum("hqk,khd->qhd", grad_scores, key_heads, preferred_element_type=jnp.float32)
        * scale
    )
    grad_keys = (
        jnp.einsum("hqk,qhd->khd", grad_scores, query_heads, preferred_element_type=jnp.float32)
        * scale
    )
    return (
        grad_queries.reshape(slot_total, -1),
        grad_keys.reshape(key_total, -1),
        grad_values.reshape(key_total, -1),
    )


def per_device(
    activations,
    slot_counts,
    qkv_weight,
    proj_weight,
    up_weight,
    down_weight,
    norm_gains,
    row_biases,
    head_biases,
    hidden_bias,
    cotangent,
):
    images, slots, width = activations.shape
    n_ctx = lax.axis_size("ctx")
    n_tp = lax.axis_size("tp")
    row_count = images * slots
    quarter = row_count // n_tp
    row_start = lax.axis_index("tp") * quarter

    def own_rows(values):
        return lax.dynamic_slice_in_dim(values, row_start, quarter, 0)

    gathered = (
        lax.all_gather(qkv_weight, "shard", axis=1, tiled=True),
        lax.all_gather(proj_weight, "shard", axis=1, tiled=True),
        lax.all_gather(up_weight, "shard", axis=0, tiled=True),
        lax.all_gather(down_weight, "shard", axis=1, tiled=True),
        lax.all_gather(norm_gains, "shard", axis=1, tiled=True),
        lax.all_gather(row_biases, "shard", axis=1, tiled=True),
    )
    qkv_full, proj_full, up_full, down_full, gains_full, shifts_full = gathered
    gains = gains_full.astype(jnp.float32)
    shifts = shifts_full.astype(jnp.float32)
    ctx_rank = lax.axis_index("ctx")
    rank_ids = jnp.arange(n_ctx, dtype=jnp.int32)
    own_count = jnp.sum(jnp.where(rank_ids[None, :] == ctx_rank, slot_counts, 0), axis=1)
    slot_ids = jnp.arange(slots, dtype=jnp.int32)
    row_valid = (slot_ids[None, :] < own_count[:, None]).reshape(row_count, 1)
    share_valid = own_rows(row_valid)
    key_valid = jnp.repeat(slot_counts, slots, axis=1) > jnp.tile(slot_ids, n_ctx)[None, :]
    act_in = activations.reshape(row_count, width).astype(jnp.float32)
    normed, norm_one_back = jax.vjp(layer_norm, act_in, gains[0], shifts[0])
    normed_low = normed.astype(jnp.bfloat16)
    projected = jnp.einsum("rd,kde->kre", normed_low, qkv_full, preferred_element_type=jnp.float32)
    biases = head_biases.astype(jnp.float32)
    queries = (projected[0] + biases[0]).astype(jnp.bfloat16).reshape(images, slots, -1)
    keys = projected[1].astype(jnp.bfloat16).reshape(images, slots, -1)
    values = (projected[2] + biases[1]).astype(jnp.bfloat16).reshape(images, slots, -1)
    keys_all, values_all = (
        lax.all_gather(keys, "ctx", axis=1, tiled=True),
        lax.all_gather(values, "ctx", axis=1, tiled=True),
    )
    mixed, log_totals = lax.map(attend, (queries, keys_all, values_all, key_valid))
    mixed_flat = mixed.reshape(row_count, -1)
    attn_part = jnp.dot(mixed_flat, proj_full, preferred_element_type=jnp.float32)
    attn_sum = lax.psum(attn_part, "tp")
    middle_full = act_in + attn_sum + shifts[2]
    normed_two, norm_two_back = jax.vjp(layer_norm, middle_full, gains[1], shifts[1])
    normed_two_low = normed_two.astype(jnp.bfloat16)
    middle = own_rows(middle_full)
    hidden = jnp.dot(
        normed_two_low, up_full, preferred_element_type=jnp.float32
    ) + hidden_bias.astype(jnp.float32)
    gelu_out, gelu_back = jax.vjp(exact_gelu, hidden)
    gelu_low = gelu_out.astype(jnp.bfloat16)
    mlp_part = jnp.dot(gelu_low, down_full, preferred_element_type=jnp.float32)
    mlp_sum = own_rows(lax.psum(mlp_part.astype(jnp.bfloat16), "tp").astype(jnp.float32))
    layer_out = (
        jnp.where(share_valid, middle + mlp_sum + shifts[3], 0.0)
        .astype(jnp.bfloat16)
        .reshape(images, quarter, width)
    )
    qkv_use, proj_use, up_use, down_use = (qkv_full, proj_full, up_full, down_full)
    grad_out = jnp.where(row_valid, cotangent.reshape(row_count, width).astype(jnp.float32), 0.0)
    grad_branch = grad_out.astype(jnp.bfloat16)
    down_grad = jnp.einsum("rf,rd->fd", gelu_low, grad_branch, preferred_element_type=jnp.float32)
    grad_gelu = jnp.einsum("rd,fd->rf", grad_branch, down_use, preferred_element_type=jnp.float32)
    (grad_hidden,) = gelu_back(grad_gelu)
    grad_hidden_low = grad_hidden.astype(jnp.bfloat16)
    up_grad = jnp.einsum(
        "rd,rf->df", normed_two_low, grad_hidden_low, preferred_element_type=jnp.float32
    )
    hidden_grad = jnp.sum(grad_hidden_low.astype(jnp.float32), axis=0)
    grad_normed_part = jnp.einsum(
        "rf,df->rd", grad_hidden_low, up_use, preferred_element_type=jnp.float32
    )
    grad_normed_two = lax.psum(grad_normed_part, "tp")
    grad_middle_norm, gain_two_grad, shift_two_grad = norm_two_back(grad_normed_two)
    grad_middle_full = grad_out + grad_middle_norm
    grad_attn = grad_middle_full.astype(jnp.bfloat16)
    grad_middle = own_rows(grad_middle_full)
    proj_grad = jnp.einsum("re,rd->ed", mixed_flat, grad_attn, preferred_element_type=jnp.float32)
    grad_mixed = (
        jnp.einsum("rd,ed->re", grad_attn, proj_use, preferred_element_type=jnp.float32)
        .astype(jnp.bfloat16)
        .reshape(images, slots, -1)
    )
    grad_queries, grad_keys_part, grad_values_part = lax.map(
        attend_back, (queries, keys_all, values_all, key_valid, log_totals, grad_mixed)
    )
    grad_keys, grad_values = (
        lax.psum_scatter(grad_keys_part, "ctx", scatter_dimension=1, tiled=True),
        lax.psum_scatter(grad_values_part, "ctx", scatter_dimension=1, tiled=True),
    )
    stacked = jnp.stack(
        [
            grad_queries.reshape(row_count, -1),
            grad_keys.reshape(row_count, -1),
            grad_values.reshape(row_count, -1),
        ]
    ).astype(jnp.bfloat16)
    qkv_grad = jnp.einsum("rd,kre->kde", normed_low, stacked, preferred_element_type=jnp.float32)
    stacked_wide = stacked.astype(jnp.float32)
    head_grad = jnp.stack([jnp.sum(stacked_wide[0], axis=0), jnp.sum(stacked_wide[2], axis=0)])
    grad_normed_one_part = jnp.einsum(
        "kre,kde->rd", stacked, qkv_use, preferred_element_type=jnp.float32
    )
    grad_normed_one = lax.psum(grad_normed_one_part, "tp")
    grad_input_norm_full, gain_one_grad, shift_one_grad = norm_one_back(grad_normed_one)
    grad_input_norm = own_rows(grad_input_norm_full)
    gains_grad = jnp.stack([gain_one_grad, gain_two_grad])
    norm_shift_grads = jnp.stack([shift_one_grad, shift_two_grad])
    input_grad = (
        (grad_middle + grad_input_norm).astype(jnp.bfloat16).reshape(images, quarter, width)
    )
    shifts_grad = jnp.concatenate(
        [
            norm_shift_grads,
            jnp.stack(
                [
                    jnp.sum(grad_attn.astype(jnp.float32), axis=0),
                    jnp.sum(grad_branch.astype(jnp.float32), axis=0),
                ]
            ),
        ],
        axis=0,
    )
    summed = lax.psum((qkv_grad, proj_grad, up_grad, down_grad, gains_grad, shifts_grad), "ctx")
    owned = (
        lax.psum_scatter(summed[0], "shard", scatter_dimension=1, tiled=True),
        lax.psum_scatter(summed[1], "shard", scatter_dimension=1, tiled=True),
        lax.psum_scatter(summed[2], "shard", scatter_dimension=0, tiled=True),
        lax.psum_scatter(summed[3], "shard", scatter_dimension=1, tiled=True),
        lax.psum_scatter(summed[4], "shard", scatter_dimension=1, tiled=True),
        lax.psum_scatter(summed[5], "shard", scatter_dimension=1, tiled=True),
    )
    bias_totals = lax.psum((head_grad, hidden_grad), ("shard", "ctx"))
    return (
        layer_out,
        input_grad,
        owned[0],
        owned[1],
        owned[2],
        owned[3],
        owned[4],
        owned[5],
        bias_totals[0],
        bias_totals[1],
    )


def solution(mesh):
    placed = (
        P("shard", "ctx", None),
        P("shard", None),
        P(None, "shard", "tp"),
        P("tp", "shard"),
        P("shard", "tp"),
        P("tp", "shard"),
        P(None, "shard"),
        P(None, "shard"),
        P(None, "tp"),
        P("tp"),
        P("shard", "ctx", None),
    )
    return jax.shard_map(
        per_device,
        mesh=mesh,
        in_specs=placed,
        out_specs=(
            P("shard", ("ctx", "tp"), None),
            P("shard", ("ctx", "tp"), None),
            P(None, "shard", "tp"),
            P("tp", "shard"),
            P("shard", "tp"),
            P("tp", "shard"),
            P(None, "shard"),
            P(None, "shard"),
            P(None, "tp"),
            P("tp"),
        ),
        check_vma=False,
    )
```

profile of v0, /device:TPU:0, one launch (start us, length us, event | category | flops | bytes accessed | tf_op | source)
XLA Modules:
  0.0 542.7 jit_solution(16820646463041530862)
XLA Ops:
  10.4 12.8 %all-gather = bf16[4,192,2]{1,2,0:T(2,128)(2,1)S(1)} all-gather(bf16[1,192,2]{1,2,0:T(2,128)(2,1)} %bitcast.183), channel_id=1, replica_groups=mesh['shard'=4,'ctx'=2,'tp'=4] {'shard'}, dimensions={0}, use_global_device_ids=true | all-gather | bytes 3840 | tf_op jit(solution)/shard_map/all_gather | solution.py:107
  23.4 1.3 convert_reduce_fusion
  24.7 1.5 fusion.12
  26.3 11.9 %all-gather.1 = bf16[4,192,4]{1,2,0:T(4,128)(2,1)S(1)} all-gather(bf16[1,192,4]{1,2,0:T(4,128)(2,1)S(1)} %bitcast.182), channel_id=1, replica_groups=mesh['shard'=4,'ctx'=2,'tp'=4] {'shard'}, dimensions={0}, use_global_device_ids=true | all-gather | bytes 7680 | tf_op jit(solution)/shard_map/all_gather | solution.py:108
  38.4 15.8 %all_gather.29 = bf16[192,768]{0,1:T(8,128)(2,1)} all-gather(bf16[192,192]{0,1:T(8,128)(2,1)S(1)} %copy.48), channel_id=1, replica_groups=mesh['shard'=4,'ctx'=2,'tp'=4] {'shard'}, dimensions={1}, use_global_device_ids=true | all-gather | bytes 368640 | tf_op jit(solution)/shard_map/all_gather | solution.py:104
  54.5 22.9 %all_gather.26 = bf16[3,768,192]{2,0,1:T(4,128)(2,1)S(1)} all-gather(bf16[3,192,192]{2,0,1:T(4,128)(2,1)S(1)} %copy.42), channel_id=1, replica_groups=mesh['shard'=4,'ctx'=2,'tp'=4] {'shard'}, dimensions={1}, use_global_device_ids=true | all-gather | bytes 1105920 | tf_op jit(solution)/shard_map/all_gather | solution.py:103
  81.4 11.9 %all_gather.28 = bf16[1,1040,192]{2,0,1:T(2,128)(2,1)S(1)} all-gather(bf16[1,520,192]{2,0,1:T(2,128)(2,1)S(1)} %copy.46), channel_id=1, replica_groups=mesh['shard'=4,'ctx'=2,'tp'=4] {'ctx'}, dimensions={1}, use_global_device_ids=true | all-gather | bytes 599040 | tf_op jit(solution)/shard_map/all_gather | solution.py:129
  93.3 2.6 copy.47
  95.9 1.8 copy.44
  97.7 9.9 %all_gather.27 = bf16[1,1040,192]{2,0,1:T(2,128)(2,1)S(1)} all-gather(bf16[1,520,192]{2,0,1:T(2,128)(2,1)S(1)} %copy.44), channel_id=1, replica_groups=mesh['shard'=4,'ctx'=2,'tp'=4] {'ctx'}, dimensions={1}, use_global_device_ids=true | all-gather | bytes 599040 | tf_op jit(solution)/shard_map/all_gather | solution.py:130
  107.7 2.6 copy.45
  110.3 1.5 fusion.56
  111.9 1.4 exponential_reduce_fusion
  113.2 1.6 copy-done
  114.8 1.4 convolution_convert_fusion.2
  116.2 1.6 fusion.57
  120.6 39.9 %all-reduce.9.cloned.1.call-done = f32[520,768]{1,0:T(8,128)} async-done(((f32[520,768]{1,0:T(8,128)}), f32[520,768]{1,0:T(8,128)}) %all-reduce.9.cloned.1.call-update) | async-done | bytes 1597456 | tf_op jit(solution)/shard_map/psum | solution.py:135
  160.5 1.7 fusion.53
  162.6 6.9 %multiply_convert_fusion.1 = (bf16[520,768]{1,0:T(8,128)(2,1)}, f32[520,768]{1,0:T(8,128)}, f32[520,768]{1,0:T(8,128)}) fusion(f32[768]{0:T(1024)S(1)} %convert_element_type.113, bf16[768,768]{1,0:T(8,128)(2,1)} %all-gather.5.cloned.1.call-done, f32[520,768]{1,0:T(8,128)S(1)} %get-tuple-element.132, f32[768]{0:T(1024)S(1)} %get-tuple-element.110, ...), kind=kOutput, calls=%fused_computation.36 | convolution fusion | flops 641771520 | bytes 6784064 | tf_op jit(solution)/shard_map/dot_general | solution.py:140
  169.6 10.6 %all-gather.7.cloned.1.call-done = bf16[768,768]{0,1:T(8,128)(2,1)} async-done(((bf16[768,192]{0,1:T(8,128)(2,1)}), bf16[768,768]{0,1:T(8,128)(2,1)}) %all-gather.7.cloned.1.call-update) | async-done | bytes 1179664 | tf_op jit(solution)/shard_map/all_gather | solution.py:106
  180.2 3.8 convert_reduce_fusion.1
  184.9 2.0 fusion.58
  186.9 42.7 %all-reduce.13.cloned.1.call-done = f32[520,768]{1,0:T(8,128)} async-done(((f32[520,768]{1,0:T(8,128)}), f32[520,768]{1,0:T(8,128)}) %all-reduce.13.cloned.1.call-update) | async-done | bytes 1597456 | tf_op jit(solution)/shard_map/psum | solution.py:166
  229.6 2.3 multiply_reduce_fusion.1
  231.9 2.2 fusion.51
  234.6 1.1 copy-done.3
  236.3 2.5 fusion.24
  238.8 4.8 multiply_reduce_fusion
  243.6 3.7 copy.53
  247.3 2.3 copy.68
  249.7 6.0 %multiply_convert_fusion = bf16[3,520,1040]{2,1,0:T(8,128)(2,1)S(1)} fusion(f32[3,520,1040]{2,1,0:T(8,128)} %get-tuple-element.140, f32[3,520,1040]{2,1,0:T(8,128)} %copy-done, f32[3,520]{1,0:T(4,128)S(1)} %get-tuple-element.139, f32[3,520]{1,0:T(4,128)S(1)} %log_add_fusion), kind=kLoop, calls=%fused_computation | loop fusion | flops 6489600 | bytes 16236480 | tf_op jit(solution)/shard_map/while/body/eval_jaxpr/convert_element_type | solution.py:63
  255.7 2.1 convolution_multiply_fusion
  257.8 3.3 copy.51
  261.1 1.0 copy.69
  262.4 3.4 fusion.23
  265.8 4.5 reduce-scatter.27.cloned.1.call-done
  270.3 1.4 reshape_bitcast_fusion
  272.6 20.4 %reduce-scatter.25.cloned.1.call-done = f32[520,192]{1,0:T(8,128)} async-done(((f32[1040,192]{1,0:T(8,128)}), f32[520,192]{1,0:T(8,128)}) %reduce-scatter.25.cloned.1.call-update) | async-done | bytes 399376
  293.0 1.4 reshape_bitcast_fusion.1
  294.4 1.4 copy.52
  295.8 3.4 convolution_bitcast_fusion.1
  300.2 2.9 convolution_bitcast_fusion.2
  303.1 2.4 convolution_bitcast_fusion
  305.5 4.2 copy.55
  309.7 4.7 reshape.243
  314.6 4.1 fusion.48
  318.7 4.1 fusion.39
  322.8 3.2 convolution_convert_fusion
  326.2 16.6 %all-reduce.15.cloned.1.call-done = f32[520,768]{1,0:T(8,128)} async-done(((f32[520,768]{1,0:T(8,128)}), f32[520,768]{1,0:T(8,128)}) %all-reduce.15.cloned.1.call-update) | async-done | bytes 1597456 | tf_op jit(solution)/shard_map/psum | solution.py:197
  342.8 2.2 fusion.11
  347.1 1.7 copy.58
  348.8 20.7 %reduce-scatter.29.cloned.1.call-done = f32[192,576]{1,0:T(8,128)} async-done(((f32[768,576]{1,0:T(8,128)}), f32[192,576]{1,0:T(8,128)}) %reduce-scatter.29.cloned.1.call-update) | async-done | bytes 442384
  369.5 1.4 reshape.244
  370.9 1.1 copy.56
  372.0 46.6 %reduce-scatter.21.cloned.1.call-done = f32[192,768]{1,0:T(8,128)} async-done(((f32[768,768]{1,0:T(8,128)}), f32[192,768]{1,0:T(8,128)}) %reduce-scatter.21.cloned.1.call-update) | async-done | bytes 589840 | tf_op jit(solution)/shard_map/reduce_scatter | solution.py:221
  418.6 49.6 %reduce-scatter.23.cloned.1.call-done = f32[768,192]{0,1:T(8,128)} async-done(((f32[768,768]{0,1:T(8,128)}), f32[768,192]{0,1:T(8,128)}) %reduce-scatter.23.cloned.1.call-update) | async-done | bytes 589840 | tf_op jit(solution)/shard_map/reduce_scatter | solution.py:222
  468.9 1.8 fusion.31
  471.0 21.1 %all-reduce = (f32[2,192]{1,0:T(2,128)}, f32[768]{0:T(1024)}) all-reduce(f32[2,192]{1,0:T(2,128)S(1)} %pad_maximum_fusion.3, f32[768]{0:T(1024)S(1)} %get-tuple-element.141), channel_id=1, replica_groups=mesh['shard'=4,'ctx'=2,'tp'=4] {'shard','ctx'}, use_global_device_ids=true, to_apply=%region_38.39 | all-reduce | flops 1152 | bytes 9216 | tf_op jit(solution)/shard_map/psum | solution.py:226
  493.0 1.8 fusion.32
  495.8 17.1 %reduce-scatter.35.cloned.1.call-done = f32[192,4]{1,0:T(8,128)} async-done(((f32[768,4]{1,0:T(8,128)}), f32[192,4]{1,0:T(8,128)}) %reduce-scatter.35.cloned.1.call-update) | async-done | bytes 3088
  513.8 5.7 %all-reduce.1 = (f32[2,192]{1,0:T(2,128)}, f32[4,192]{1,0:T(4,128)}) all-reduce(f32[2,192]{1,0:T(2,128)S(1)} %copy.60, f32[4,192]{1,0:T(4,128)S(1)} %copy.62), channel_id=1, replica_groups=mesh['shard'=4,'ctx'=2,'tp'=4] {'ctx'}, use_global_device_ids=true, to_apply=%region_28.29 | all-reduce | flops 1152 | bytes 9216 | tf_op jit(solution)/shard_map/psum | solution.py:217
  519.5 10.2 %all-reduce.17.cloned.1.call-done = (f32[3,192,192]{1,2,0:T(8,128)}, f32[192,192]{1,0:T(8,128)}, f32[192,768]{1,0:T(8,128)}, f32[768,192]{0,1:T(8,128)}) async-done(((f32[3,192,192]{1,2,0:T(8,128)}, f32[192,192]{1,0:T(8,128)}, f32[192,768]{1,0:T(8,128)}, f32[768,192]{0,1:T(8,128)}), (f32[3,192,192]{1,2,0:T(8,128)}, f32[192,192]{1,0:T(8,128)}, f32[192,768]{1,0:T(8,128)}, ...) | async-done | bytes 1769488 | tf_op jit(solution)/shard_map/psum | solution.py:217
  529.8 2.2 copy.50
  532.0 1.6 copy.78
  (142 shorter events, 21.8 us)
Async XLA Ops:
  8.0 18.3 %copy-start.20 = (bf16[4,192]{1,0:T(4,128)(2,1)S(1)}, bf16[4,192]{1,0:T(4,128)(2,1)}, u32[]{:S(2)}) copy-start(bf16[4,192]{1,0:T(4,128)(2,1)} %param.18) | copy-start | bytes 4612
  8.0 30.3 %copy-start.19 = (bf16[192,192]{1,0:T(8,128)(2,1)S(1)}, bf16[192,192]{1,0:T(8,128)(2,1)}, u32[]{:S(2)}) copy-start(bf16[192,192]{1,0:T(8,128)(2,1)} %param.14) | copy-start | bytes 221188
  8.0 46.2 %copy-start.18 = (bf16[3,192,192]{2,1,0:T(8,128)(2,1)S(1)}, bf16[3,192,192]{2,1,0:T(8,128)(2,1)}, u32[]{:S(2)}) copy-start(bf16[3,192,192]{2,1,0:T(8,128)(2,1)} %param.13) | copy-start | bytes 663556
  8.0 152.5 %all-reduce.9.cloned.1.call-start = ((), (), s32[]{:S(2)}) async-start(), calls=%async_computation.8 | async-start | bytes 3194880 | tf_op jit(solution)/shard_map/psum | solution.py:135
  77.4 1.1 copy-start.2
  78.3 1.3 copy-start.14
  95.9 14.4 %copy-start.5 = (bf16[1,1040,192]{1,2,0:T(8,128)(2,1)}, bf16[1,1040,192]{1,2,0:T(8,128)(2,1)S(1)}, u32[]{:S(2)}) copy-start(bf16[1,1040,192]{1,2,0:T(8,128)(2,1)S(1)} %copy.47) | copy-start | bytes 1198084
  111.9 3.0 copy-start
  114.8 1.4 copy-start.6
  116.2 1.7 copy-start.8
  117.9 1.4 copy-start.22
  117.9 2.7 copy-start.21
  117.9 44.7 %all-gather.5.cloned.1.call-start = ((), (), s32[]{:S(2)}) async-start(), calls=%async_computation.9 | async-start | bytes 1474560 | tf_op jit(solution)/shard_map/all_gather | solution.py:105
  118.5 61.7 %all-gather.7.cloned.1.call-start = ((), (), s32[]{:S(2)}) async-start(), calls=%async_computation.10 | async-start | bytes 1474560 | tf_op jit(solution)/shard_map/all_gather | solution.py:106
  119.1 110.5 %all-reduce.13.cloned.1.call-start = ((), (), s32[]{:S(2)}) async-start(), calls=%async_computation.12 | async-start | bytes 3194880 | tf_op jit(solution)/shard_map/psum | solution.py:166
  180.2 4.7 copy-start.23
  184.0 0.9 copy-start.24
  186.9 83.4 %reduce-scatter.27.cloned.1.call-start = ((), (), s32[]{:S(2)}) async-start(), calls=%async_computation.17 | async-start | bytes 1597440
  229.6 6.7 %slice-start = ((s8[7188480]{0:T(1024)(128)(4,1)}), s8[4194304]{0:T(1024)(128)(4,1)S(1)}, s32[]{:S(2)}) async-start(s8[7188480]{0:T(1024)(128)(4,1)} %bitcast.146), calls=%async_computation.23 | async-start | bytes 8388608
  231.9 2.3 copy-start.15
  231.9 4.4 slice-start.1
  234.1 1.6 copy-start.7
  234.6 1.2 copy-start.3
  249.7 43.4 %reduce-scatter.25.cloned.1.call-start = ((), (), s32[]{:S(2)}) async-start(), calls=%async_computation.16 | async-start | bytes 1597440
  255.7 2.1 copy-start.1
  262.1 80.6 %all-reduce.15.cloned.1.call-start = ((), (), s32[]{:S(2)}) async-start(), calls=%async_computation.13 | async-start | bytes 3194880 | tf_op jit(solution)/shard_map/psum | solution.py:197
  272.6 30.5 %copy-start.10 = (bf16[1,520,192]{1,2,0:T(8,128)(2,1)}, bf16[1,520,192]{1,2,0:T(8,128)(2,1)S(1)}, u32[]{:S(2)}) copy-start(bf16[1,520,192]{1,2,0:T(8,128)(2,1)S(1)} %copy.54) | copy-start | bytes 599044
  299.2 0.9 copy-start.9
  299.2 3.9 copy-start.12
  299.2 47.8 %reduce-scatter.31.cloned.1.call-start = ((), (), s32[]{:S(2)}) async-start(), calls=%async_computation.19 | async-start | bytes 983040
  303.0 66.4 %reduce-scatter.29.cloned.1.call-start = ((), (), s32[]{:S(2)}) async-start(), calls=%async_computation.18 | async-start | bytes 2457600
  314.5 104.1 %reduce-scatter.21.cloned.1.call-start = ((), (), s32[]{:S(2)}) async-start(), calls=%async_computation.14 | async-start | bytes 2949120 | tf_op jit(solution)/shard_map/reduce_scatter | solution.py:221
  318.6 149.6 %reduce-scatter.23.cloned.1.call-start = ((), (), s32[]{:S(2)}) async-start(), calls=%async_computation.15 | async-start | bytes 2949120 | tf_op jit(solution)/shard_map/reduce_scatter | solution.py:222
  322.8 146.1 %all-reduce.11.cloned.1.call-start = ((), (), s32[]{:S(2)}) async-start(), calls=%async_computation.11 | async-start | bytes 1597440 | tf_op jit(solution)/shard_map/psum | solution.py:146
  326.1 168.7 %reduce-scatter.33.cloned.1.call-start = ((), (), s32[]{:S(2)}) async-start(), calls=%async_computation.20 | async-start | bytes 491520
  346.0 166.9 %reduce-scatter.35.cloned.1.call-start = ((), (), s32[]{:S(2)}) async-start(), calls=%async_computation.21 | async-start | bytes 491520
  347.0 182.7 %all-reduce.17.cloned.1.call-start = ((), (), s32[]{:S(2)}) async-start(), calls=%async_computation.22 | async-start | bytes 3932160 | tf_op jit(solution)/shard_map/psum | solution.py:217
  372.0 98.7 %copy-start.11 = (bf16[1,520,192]{1,2,0:T(8,128)(2,1)S(1)}, bf16[1,520,192]{1,2,0:T(8,128)(2,1)}, u32[]{:S(2)}) copy-start(bf16[1,520,192]{1,2,0:T(8,128)(2,1)} %copy-done.10) | copy-start | bytes 599044
  372.0 98.7 %copy-start.13 = (bf16[1,520,192]{1,2,0:T(8,128)(2,1)S(1)}, bf16[1,520,192]{1,2,0:T(8,128)(2,1)}, u32[]{:S(2)}) copy-start(bf16[1,520,192]{1,2,0:T(8,128)(2,1)} %copy.52) | copy-start | bytes 599044
  470.7 21.5 %copy-start.4 = (f32[520,768]{1,0:T(8,128)S(1)}, f32[520,768]{1,0:T(8,128)}, u32[]{:S(2)}) copy-start(f32[520,768]{1,0:T(8,128)} %all-reduce.15.cloned.1.call-done) | copy-start | bytes 4792324
  529.7 3.8 copy-start.17
  529.8 4.7 copy-start.16
Sparse Core Ops, SparseCore 0:
  118.0 42.4 all-reduce.8
  187.0 42.5 all-reduce.12
  249.8 20.4 reduce-scatter.26
  272.5 20.4 reduce-scatter.24
  299.4 43.3 all-reduce.14
  345.0 34.5 all-reduce.10
  468.3 61.3 all-reduce.16
Sparse Core Ops, SparseCore 1:
  120.0 29.3 all-gather.4
  150.7 29.4 all-gather.6
  303.1 23.0 reduce-scatter.30
  328.5 40.9 reduce-scatter.28
  371.8 46.7 reduce-scatter.20
  420.9 47.2 reduce-scatter.22
  471.0 20.1 reduce-scatter.32
  493.9 18.9 reduce-scatter.34
where the time goes:
time: 544 us; the launch traced here: 543 us
  waiting for transfers between devices  280 us (51%)
  blocking collectives  112 us (21%)
  local copies, waits for them, and re-layouts  53.1 us (10%)
  matrix products  51.7 us (10%)
  other arithmetic  28.1 us (5%)
  between operations  16.2 us (3%)
    unnamed x21, waiting for transfers between devices  63.9 us
    reduce_scatter x1, waiting for transfers between devices, per_device(): lax.psum_scatter(summed[3], 'shard', scatter_dimension=1, tiled=True)  49.6 us
    reduce_scatter x1, waiting for transfers between devices, per_device(): lax.psum_scatter(summed[2], 'shard', scatter_dimension=0, tiled=True)  46.6 us
    unnamed x77, local copies, waits for them, and re-layouts  43 us
    psum x1, waiting for transfers between devices, per_device(): grad_normed_two = lax.psum(grad_normed_part, 'tp')  42.7 us
    psum x1, waiting for transfers between devices, per_device(): attn_sum = lax.psum(attn_part, 'tp')  39.9 us
    all_gather x1, blocking collectives, per_device(): lax.all_gather(qkv_weight, 'shard', axis=1, tiled=True)  22.9 us
    psum x1, blocking collectives, per_device(): bias_totals = lax.psum((head_grad, hidden_grad), ('shard', 'ctx'))  21.1 us
  transfers between devices with their start and end apart: 15, of which 11 were waited for; matrix products, arithmetic and copies ran while one was open for 13% of the time, Pallas kernels for 0%

commit v1 on v0

--- a/solution.py
+++ b/solution.py
@@ -132,7 +132,7 @@
     mixed, log_totals = lax.map(attend, (queries, keys_all, values_all, key_valid))
     mixed_flat = mixed.reshape(row_count, -1)
     attn_part = jnp.dot(mixed_flat, proj_full, preferred_element_type=jnp.float32)
-    attn_sum = lax.psum(attn_part, "tp")
+    attn_sum = jnp.sum(lax.all_gather(attn_part, "tp"), axis=0)
     middle_full = act_in + attn_sum + shifts[2]
     normed_two, norm_two_back = jax.vjp(layer_norm, middle_full, gains[1], shifts[1])
     normed_two_low = normed_two.astype(jnp.bfloat16)

time: 544 us -> 714 us (1.31)
  waiting for transfers between devices: 280 us -> 447 us
    psum x1, waiting for transfers between devices: 10.2 us -> 55.3 us  [per_device(): lax.psum((qkv_grad, proj_grad, up_grad, down_grad, gains_grad, shifts_gra...]
    all_gather x0 -> x1, waiting for transfers between devices: none -> 43.2 us  [per_device(): attn_sum = jnp.sum(lax.all_gather(attn_part, 'tp'), axis=0)]
    unnamed x21, waiting for transfers between devices: 63.9 us -> 107 us
    psum x1 -> x0, waiting for transfers between devices: 39.9 us -> none  [per_device(): attn_sum = lax.psum(attn_part, 'tp')]
    psum x1, waiting for transfers between devices: 0.02 us -> 35.6 us  [per_device(): lax.psum(mlp_part.astype(jnp.bfloat16), 'tp').astype(jnp.float32)]
    all_gather x1, waiting for transfers between devices: 0.03 us -> 25.4 us  [per_device(): lax.all_gather(up_weight, 'shard', axis=0, tiled=True)]
    all_gather x1, waiting for transfers between devices: 10.6 us -> 24.3 us  [per_device(): lax.all_gather(down_weight, 'shard', axis=1, tiled=True)]
  transfers between devices with their start and end apart: 15 -> 15, of which waited for: 11 -> 14; matrix products, arithmetic and copies ran while one was open for 13% -> 10% of each run, Pallas kernels for 0% -> 0%
where the time goes in v1:
time: 714 us; the launch traced here: 713 us
  waiting for transfers between devices  447 us (63%)
  blocking collectives  113 us (16%)
  local copies, waits for them, and re-layouts  53.1 us (7%)
  matrix products  51.6 us (7%)
  other arithmetic  32.6 us (5%)
  between operations  14.5 us (2%)
    unnamed x21, waiting for transfers between devices  107 us
    psum x1, waiting for transfers between devices, per_device(): lax.psum((qkv_grad, proj_grad, up_grad, down_grad, gains_grad, shifts_gra...  55.3 us
    reduce_scatter x1, waiting for transfers between devices, per_device(): lax.psum_scatter(summed[3], 'shard', scatter_dimension=1, tiled=True)  49.9 us
    reduce_scatter x1, waiting for transfers between devices, per_device(): lax.psum_scatter(summed[2], 'shard', scatter_dimension=0, tiled=True)  47 us
    all_gather x1, waiting for transfers between devices, per_device(): attn_sum = jnp.sum(lax.all_gather(attn_part, 'tp'), axis=0)  43.2 us
    unnamed x77, local copies, waits for them, and re-layouts  43 us
    psum x1, waiting for transfers between devices, per_device(): grad_normed_two = lax.psum(grad_normed_part, 'tp')  42.6 us
    psum x1, waiting for transfers between devices, per_device(): lax.psum(mlp_part.astype(jnp.bfloat16), 'tp').astype(jnp.float32)  35.6 us
  transfers between devices with their start and end apart: 15, of which 14 were waited for; matrix products, arithmetic and copies ran while one was open for 10% of the time, Pallas kernels for 0%

profile of v1, /device:TPU:0, one launch (start us, length us, event | category | flops | bytes accessed | tf_op | source)
XLA Modules:
  0.0 713.0 jit_solution(1997354477658053114)
XLA Ops:
  9.6 12.8 %all-gather.1 = bf16[4,192,2]{1,2,0:T(2,128)(2,1)S(1)} all-gather(bf16[1,192,2]{1,2,0:T(2,128)(2,1)} %bitcast.185), channel_id=1, replica_groups=mesh['shard'=4,'ctx'=2,'tp'=4] {'shard'}, dimensions={0}, use_global_device_ids=true | all-gather | bytes 3840 | tf_op jit(solution)/shard_map/all_gather | solution.py:107
  23.9 1.5 fusion.12
  25.5 11.9 %all-gather.2 = bf16[4,192,4]{1,2,0:T(4,128)(2,1)S(1)} all-gather(bf16[1,192,4]{1,2,0:T(4,128)(2,1)S(1)} %bitcast.184), channel_id=1, replica_groups=mesh['shard'=4,'ctx'=2,'tp'=4] {'shard'}, dimensions={0}, use_global_device_ids=true | all-gather | bytes 7680 | tf_op jit(solution)/shard_map/all_gather | solution.py:108
  37.6 15.8 %all_gather.35 = bf16[192,768]{0,1:T(8,128)(2,1)} all-gather(bf16[192,192]{0,1:T(8,128)(2,1)S(1)} %copy.48), channel_id=1, replica_groups=mesh['shard'=4,'ctx'=2,'tp'=4] {'shard'}, dimensions={1}, use_global_device_ids=true | all-gather | bytes 368640 | tf_op jit(solution)/shard_map/all_gather | solution.py:104
  53.7 22.9 %all_gather.32 = bf16[3,768,192]{2,0,1:T(4,128)(2,1)S(1)} all-gather(bf16[3,192,192]{2,0,1:T(4,128)(2,1)S(1)} %copy.42), channel_id=1, replica_groups=mesh['shard'=4,'ctx'=2,'tp'=4] {'shard'}, dimensions={1}, use_global_device_ids=true | all-gather | bytes 1105920 | tf_op jit(solution)/shard_map/all_gather | solution.py:103
  80.5 11.9 %all_gather.34 = bf16[1,1040,192]{2,0,1:T(2,128)(2,1)S(1)} all-gather(bf16[1,520,192]{2,0,1:T(2,128)(2,1)S(1)} %copy.46), channel_id=1, replica_groups=mesh['shard'=4,'ctx'=2,'tp'=4] {'ctx'}, dimensions={1}, use_global_device_ids=true | all-gather | bytes 599040 | tf_op jit(solution)/shard_map/all_gather | solution.py:129
  92.4 2.6 copy.47
  95.1 1.8 copy.44
  96.9 9.9 %all_gather.33 = bf16[1,1040,192]{2,0,1:T(2,128)(2,1)S(1)} all-gather(bf16[1,520,192]{2,0,1:T(2,128)(2,1)S(1)} %copy.44), channel_id=1, replica_groups=mesh['shard'=4,'ctx'=2,'tp'=4] {'ctx'}, dimensions={1}, use_global_device_ids=true | all-gather | bytes 599040 | tf_op jit(solution)/shard_map/all_gather | solution.py:130
  106.9 2.6 copy.45
  109.5 1.5 fusion.56
  111.0 1.4 exponential_reduce_fusion
  112.4 1.6 copy-done
  114.0 1.4 convolution_convert_fusion.2
  115.4 1.6 fusion.57
  120.1 43.2 %all-gather.11.cloned.1.call-done = f32[2080,768]{1,0:T(8,128)} async-done(((f32[520,768]{1,0:T(8,128)}), f32[2080,768]{1,0:T(8,128)}) %all-gather.11.cloned.1.call-update) | async-done | bytes 6389776 | tf_op jit(solution)/shard_map/all_gather | solution.py:135
  163.3 4.6 reduce_sum.197
  167.9 1.7 fusion.53
  169.9 25.4 %all-gather.7.cloned.1.call-done = bf16[768,768]{1,0:T(8,128)(2,1)} async-done(((bf16[192,768]{1,0:T(8,128)(2,1)}), bf16[768,768]{1,0:T(8,128)(2,1)}) %all-gather.7.cloned.1.call-update) | async-done | bytes 1179664 | tf_op jit(solution)/shard_map/all_gather | solution.py:105
  195.3 6.9 multiply_convert_fusion.1
  202.2 24.3 %all-gather.9.cloned.1.call-done = bf16[768,768]{0,1:T(8,128)(2,1)} async-done(((bf16[768,192]{0,1:T(8,128)(2,1)}), bf16[768,768]{0,1:T(8,128)(2,1)}) %all-gather.9.cloned.1.call-update) | async-done | bytes 1179664 | tf_op jit(solution)/shard_map/all_gather | solution.py:106
  226.5 3.8 convert_reduce_fusion.1
  231.2 2.0 fusion.58
  233.3 42.6 %all-reduce.10.cloned.1.call-done = f32[520,768]{1,0:T(8,128)} async-done(((f32[520,768]{1,0:T(8,128)}), f32[520,768]{1,0:T(8,128)}) %all-reduce.10.cloned.1.call-update) | async-done | bytes 1597456 | tf_op jit(solution)/shard_map/psum | solution.py:166
  275.8 2.3 multiply_reduce_fusion.1
  278.1 2.2 fusion.51
  282.5 2.5 fusion.24
  285.0 4.8 multiply_reduce_fusion
  289.8 3.7 copy.53
  293.6 2.3 copy.68
  295.9 6.0 multiply_convert_fusion
  301.9 2.1 convolution_multiply_fusion
  304.0 3.3 copy.51
  308.6 3.4 fusion.23
  312.0 4.5 reduce-scatter.27.cloned.1.call-done
  316.6 1.4 reshape_bitcast_fusion
  318.9 20.4 %reduce-scatter.25.cloned.1.call-done = f32[520,192]{1,0:T(8,128)} async-done(((f32[1040,192]{1,0:T(8,128)}), f32[520,192]{1,0:T(8,128)}) %reduce-scatter.25.cloned.1.call-update) | async-done | bytes 399376
  339.3 1.4 reshape_bitcast_fusion.1
  340.7 1.4 copy.52
  342.0 3.4 convolution_bitcast_fusion.1
  346.4 2.9 convolution_bitcast_fusion.2
  349.3 2.4 convolution_bitcast_fusion
  351.7 4.2 copy.55
  356.0 4.7 reshape.244
  360.8 4.0 fusion.48
  364.9 4.1 fusion.39
  369.0 3.2 convolution_convert_fusion
  372.4 16.6 %all-reduce.12.cloned.1.call-done = f32[520,768]{1,0:T(8,128)} async-done(((f32[520,768]{1,0:T(8,128)}), f32[520,768]{1,0:T(8,128)}) %all-reduce.12.cloned.1.call-update) | async-done | bytes 1597456 | tf_op jit(solution)/shard_map/psum | solution.py:197
  389.0 2.1 fusion.11
  393.2 21.4 %reduce-scatter.31.cloned.1.call-done = f32[192,192]{1,0:T(8,128)} async-done(((f32[768,192]{1,0:T(8,128)}), f32[192,192]{1,0:T(8,128)}) %reduce-scatter.31.cloned.1.call-update) | async-done | bytes 147472
  414.6 1.7 copy.58
  416.3 41.3 %reduce-scatter.29.cloned.1.call-done = f32[192,576]{1,0:T(8,128)} async-done(((f32[768,576]{1,0:T(8,128)}), f32[192,576]{1,0:T(8,128)}) %reduce-scatter.29.cloned.1.call-update) | async-done | bytes 442384
  457.7 1.4 reshape.245
  460.2 47.0 %reduce-scatter.21.cloned.1.call-done = f32[192,768]{1,0:T(8,128)} async-done(((f32[768,768]{1,0:T(8,128)}), f32[192,768]{1,0:T(8,128)}) %reduce-scatter.21.cloned.1.call-update) | async-done | bytes 589840 | tf_op jit(solution)/shard_map/reduce_scatter | solution.py:221
  507.1 49.9 %reduce-scatter.23.cloned.1.call-done = f32[768,192]{0,1:T(8,128)} async-done(((f32[768,768]{0,1:T(8,128)}), f32[768,192]{0,1:T(8,128)}) %reduce-scatter.23.cloned.1.call-update) | async-done | bytes 589840 | tf_op jit(solution)/shard_map/reduce_scatter | solution.py:222
  557.7 35.6 %all-reduce.8.cloned.1.call-done = bf16[520,768]{1,0:T(8,128)(2,1)} async-done(((bf16[520,768]{1,0:T(8,128)(2,1)}), bf16[520,768]{1,0:T(8,128)(2,1)}) %all-reduce.8.cloned.1.call-update) | async-done | bytes 798736 | tf_op jit(solution)/shard_map/psum | solution.py:146
  593.3 1.8 fusion.31
  595.4 22.4 %all-reduce = (f32[2,192]{1,0:T(2,128)}, f32[768]{0:T(1024)}) all-reduce(f32[2,192]{1,0:T(2,128)S(1)} %pad_maximum_fusion.3, f32[768]{0:T(1024)S(1)} %get-tuple-element.141), channel_id=1, replica_groups=mesh['shard'=4,'ctx'=2,'tp'=4] {'shard','ctx'}, use_global_device_ids=true, to_apply=%region_38.39 | all-reduce | flops 1152 | bytes 9216 | tf_op jit(solution)/shard_map/psum | solution.py:226
  618.6 1.8 fusion.32
  621.4 17.8 %reduce-scatter.35.cloned.1.call-done = f32[192,4]{1,0:T(8,128)} async-done(((f32[768,4]{1,0:T(8,128)}), f32[192,4]{1,0:T(8,128)}) %reduce-scatter.35.cloned.1.call-update) | async-done | bytes 3088
  640.1 5.6 all-reduce.1
  645.7 55.3 %all-reduce.14.cloned.1.call-done = (f32[3,192,192]{1,2,0:T(8,128)}, f32[192,192]{1,0:T(8,128)}, f32[192,768]{1,0:T(8,128)}, f32[768,192]{0,1:T(8,128)}) async-done(((f32[3,192,192]{1,2,0:T(8,128)}, f32[192,192]{1,0:T(8,128)}, f32[192,768]{1,0:T(8,128)}, f32[768,192]{0,1:T(8,128)}), (f32[3,192,192]{1,2,0:T(8,128)}, f32[192,192]{1,0:T(8,128)}, f32[192,768]{1,0:T(8,128)}, ...) | async-done | bytes 1769488 | tf_op jit(solution)/shard_map/psum | solution.py:217
  701.0 2.2 copy.50
  703.2 1.6 copy.77
  (143 shorter events, 26.7 us)
Async XLA Ops:
  7.2 18.3 %copy-start.20 = (bf16[4,192]{1,0:T(4,128)(2,1)S(1)}, bf16[4,192]{1,0:T(4,128)(2,1)}, u32[]{:S(2)}) copy-start(bf16[4,192]{1,0:T(4,128)(2,1)} %param.18) | copy-start | bytes 4612
  7.2 30.3 %copy-start.19 = (bf16[192,192]{1,0:T(8,128)(2,1)S(1)}, bf16[192,192]{1,0:T(8,128)(2,1)}, u32[]{:S(2)}) copy-start(bf16[192,192]{1,0:T(8,128)(2,1)} %param.14) | copy-start | bytes 221188
  7.2 46.2 %copy-start.18 = (bf16[3,192,192]{2,1,0:T(8,128)(2,1)S(1)}, bf16[3,192,192]{2,1,0:T(8,128)(2,1)}, u32[]{:S(2)}) copy-start(bf16[3,192,192]{2,1,0:T(8,128)(2,1)} %param.13) | copy-start | bytes 663556
  7.2 156.1 %all-gather.11.cloned.1.call-start = ((), (), s32[]{:S(2)}) async-start(), calls=%async_computation.13 | async-start | bytes 7987200 | tf_op jit(solution)/shard_map/all_gather | solution.py:135
  76.6 1.1 copy-start.2
  77.5 1.3 copy-start.14
  95.1 14.4 %copy-start.5 = (bf16[1,1040,192]{1,2,0:T(8,128)(2,1)}, bf16[1,1040,192]{1,2,0:T(8,128)(2,1)S(1)}, u32[]{:S(2)}) copy-start(bf16[1,1040,192]{1,2,0:T(8,128)(2,1)S(1)} %copy.47) | copy-start | bytes 1198084
  111.0 3.0 copy-start
  114.0 1.4 copy-start.6
  115.4 1.7 copy-start.8
  117.0 1.8 copy-start.22
  117.0 3.1 copy-start.21
  117.1 78.3 %all-gather.7.cloned.1.call-start = ((), (), s32[]{:S(2)}) async-start(), calls=%async_computation.8 | async-start | bytes 1474560 | tf_op jit(solution)/shard_map/all_gather | solution.py:105
  117.8 108.7 %all-gather.9.cloned.1.call-start = ((), (), s32[]{:S(2)}) async-start(), calls=%async_computation.9 | async-start | bytes 1474560 | tf_op jit(solution)/shard_map/all_gather | solution.py:106
  118.6 157.3 %all-reduce.10.cloned.1.call-start = ((), (), s32[]{:S(2)}) async-start(), calls=%async_computation.11 | async-start | bytes 3194880 | tf_op jit(solution)/shard_map/psum | solution.py:166
  226.5 4.7 copy-start.23
  230.3 0.9 copy-start.24
  233.2 83.3 %reduce-scatter.27.cloned.1.call-start = ((), (), s32[]{:S(2)}) async-start(), calls=%async_computation.17 | async-start | bytes 1597440
  275.8 6.7 slice-start
  278.1 2.3 copy-start.15
  278.1 4.4 slice-start.1
  280.4 1.6 copy-start.7
  280.8 1.2 copy-start.3
  295.9 43.4 %reduce-scatter.25.cloned.1.call-start = ((), (), s32[]{:S(2)}) async-start(), calls=%async_computation.16 | async-start | bytes 1597440
  301.9 2.1 copy-start.1
  308.4 80.6 %all-reduce.12.cloned.1.call-start = ((), (), s32[]{:S(2)}) async-start(), calls=%async_computation.12 | async-start | bytes 3194880 | tf_op jit(solution)/shard_map/psum | solution.py:197
  318.8 30.5 %copy-start.10 = (bf16[1,520,192]{1,2,0:T(8,128)(2,1)}, bf16[1,520,192]{1,2,0:T(8,128)(2,1)S(1)}, u32[]{:S(2)}) copy-start(bf16[1,520,192]{1,2,0:T(8,128)(2,1)S(1)} %copy.54) | copy-start | bytes 599044
  345.4 0.9 copy-start.9
  345.5 3.9 copy-start.12
  345.5 69.2 %reduce-scatter.31.cloned.1.call-start = ((), (), s32[]{:S(2)}) async-start(), calls=%async_computation.19 | async-start | bytes 983040
  349.3 108.4 %reduce-scatter.29.cloned.1.call-start = ((), (), s32[]{:S(2)}) async-start(), calls=%async_computation.18 | async-start | bytes 2457600
  360.7 146.4 %reduce-scatter.21.cloned.1.call-start = ((), (), s32[]{:S(2)}) async-start(), calls=%async_computation.14 | async-start | bytes 2949120 | tf_op jit(solution)/shard_map/reduce_scatter | solution.py:221
  364.8 192.2 %reduce-scatter.23.cloned.1.call-start = ((), (), s32[]{:S(2)}) async-start(), calls=%async_computation.15 | async-start | bytes 2949120 | tf_op jit(solution)/shard_map/reduce_scatter | solution.py:222
  369.0 224.4 %all-reduce.8.cloned.1.call-start = ((), (), s32[]{:S(2)}) async-start(), calls=%async_computation.10 | async-start | bytes 1597440 | tf_op jit(solution)/shard_map/psum | solution.py:146
  372.3 248.1 %reduce-scatter.33.cloned.1.call-start = ((), (), s32[]{:S(2)}) async-start(), calls=%async_computation.20 | async-start | bytes 491520
  392.1 247.1 %reduce-scatter.35.cloned.1.call-start = ((), (), s32[]{:S(2)}) async-start(), calls=%async_computation.21 | async-start | bytes 491520
  393.1 307.8 %all-reduce.14.cloned.1.call-start = ((), (), s32[]{:S(2)}) async-start(), calls=%async_computation.22 | async-start | bytes 3932160 | tf_op jit(solution)/shard_map/psum | solution.py:217
  460.1 135.0 %copy-start.11 = (bf16[1,520,192]{1,2,0:T(8,128)(2,1)S(1)}, bf16[1,520,192]{1,2,0:T(8,128)(2,1)}, u32[]{:S(2)}) copy-start(bf16[1,520,192]{1,2,0:T(8,128)(2,1)} %copy-done.10) | copy-start | bytes 599044
  460.1 135.0 %copy-start.13 = (bf16[1,520,192]{1,2,0:T(8,128)(2,1)S(1)}, bf16[1,520,192]{1,2,0:T(8,128)(2,1)}, u32[]{:S(2)}) copy-start(bf16[1,520,192]{1,2,0:T(8,128)(2,1)} %copy.52) | copy-start | bytes 599044
  595.1 22.7 %copy-start.4 = (f32[520,768]{1,0:T(8,128)S(1)}, f32[520,768]{1,0:T(8,128)}, u32[]{:S(2)}) copy-start(f32[520,768]{1,0:T(8,128)} %all-reduce.12.cloned.1.call-done) | copy-start | bytes 4792324
  701.0 3.8 copy-start.17
  701.0 4.7 copy-start.16
Sparse Core Ops, SparseCore 0:
  117.2 46.0 all-gather.10
  164.8 30.4 all-gather.6
  196.9 29.5 all-gather.8
  233.3 42.4 all-reduce.9
  296.0 20.5 reduce-scatter.26
  318.8 20.4 reduce-scatter.24
  345.6 43.3 all-reduce.11
  391.3 23.3 reduce-scatter.30
  416.9 40.6 reduce-scatter.28
  459.8 47.2 reduce-scatter.20
  509.4 47.5 reduce-scatter.22
  559.2 34.0 all-reduce.7
  596.2 21.3 reduce-scatter.32
  620.4 18.7 reduce-scatter.34
  642.1 58.8 all-reduce.13
